TPU v7x, 256 devices: a whole 4x4x8 slice. The times are simulated.
256 devices in a mesh: prow: 32 (over z_hi, y, x), pcol: 8 (over z_lo, core).
Axes of the slice: x: 4, y: 4, z: 8 (z_hi: 2, z_lo: 4; z = z_hi * 4 + z_lo), core: 2. Of those that a mesh axis runs over, the one named last changes fastest.
Arguments:
- eigen_rows: float32 [1024, 229376], P(('pcol', 'prow')), may hold values from -6 to 6
- reflectors: float32 [229376, 512], P('prow', 'pcol'), may hold values from -0.375 to 0.375
- tfactors: float32 [2, 256, 256], replicated, may hold values from -0.01171875 to 0.01171875
Outputs:
- back_rows: float32 [1024, 229376], P('pcol', 'prow')
All inputs are finite; a program needn't handle non-finite values.
Results may differ from a plain program's by a relative error of at most 0.000084.
Values sent between devices are 32-bit elements; how exact they have to be, the bound alone decides.
No kernel may reach another device: no remote copies, remote signals or barrier semaphores. Data moves between devices by JAX's collectives and lax.ppermute only.
A program may use at most 128 MiB of HBM per device.

v0:
```python
import jax
import jax.numpy as jnp
from jax import lax
from jax.sharding import PartitionSpec as P


def upper_part(square):
    width = square.shape[0]
    rows = lax.broadcasted_iota(jnp.int32, (width, width), 0)
    cols = lax.broadcasted_iota(jnp.int32, (width, width), 1)
    return jnp.where(cols >= rows, square, jnp.zeros_like(square))


def matmul(left, right):
    return jnp.dot(left, right, precision=lax.Precision.HIGHEST, preferred_element_type=jnp.float32)


def apply_both(matrix, vectors, tfactors, summer):
    width = tfactors.shape[1]
    first_tri = upper_part(tfactors[0])
    second_tri = upper_part(tfactors[1])
    for panel_index in (1, 0):
        panel_vectors = vectors[:, panel_index * width : (panel_index + 1) * width]
        triangle = second_tri if panel_index == 1 else first_tri
        projected = summer(matmul(matrix, panel_vectors))
        matrix = matrix - matmul(matmul(projected, triangle.T), panel_vectors.T)
    return matrix


def body(eigen_rows, reflectors, tfactors):
    grid_rows = lax.all_to_all(eigen_rows, "prow", split_axis=1, concat_axis=0, tiled=True)
    grid_vectors = lax.all_gather(reflectors, "pcol", axis=1, tiled=True)

    def summer_grid(values):
        return lax.psum(values, "prow")

    return apply_both(grid_rows, grid_vectors, tfactors, summer_grid)


def solution(mesh):
    return jax.shard_map(
        body,
        mesh=mesh,
        in_specs=(P(("pcol", "prow"), None), P("prow", "pcol"), P()),
        out_specs=P("pcol", "prow"),
        check_vma=False,
    )
```

profile of v0, /device:TPU:2, one launch (start us, length us, event | category | flops | bytes accessed | tf_op | source)
XLA Modules:
  0.0 1083.1 jit_solution(4444081856075703498)
XLA Ops:
  6.5 0.0 all-gather.2.cloned.1.call-start
  6.5 0.7 all-gather.2.cloned.1.call-update
  7.3 0.0 all-reduce.3.cloned.1.call-start
  7.3 137.9 %all_to_all.19 = f32[4,32,7168]{2,0,1:T(4,128)} all-to-all(f32[4,32,7168]{2,0,1:T(4,128)} %bitcast.15), channel_id=1, replica_groups=mesh['prow'=32,'pcol'=8] {'prow'}, dimensions={1} | all-to-all | bytes 7340032 | tf_op jit(solution)/shard_map/all_to_all | solution.py:31
  145.2 5.2 all_to_all.17
  150.4 0.0 copy-start.2
  150.4 90.1 %all-gather.2.cloned.1.call-done = f32[7168,512]{0,1:T(8,128)} async-done(((f32[7168,64]{0,1:T(8,128)}), f32[7168,512]{0,1:T(8,128)}) %all-gather.2.cloned.1.call-update) | async-done | bytes 14680080 | tf_op jit(solution)/shard_map/all_gather | solution.py:32
  240.5 12.3 %fusion.4 = f32[128,256]{1,0:T(8,128)} fusion(f32[128,7168]{1,0:T(8,128)} %all_to_all.17, f32[7168,512]{0,1:T(8,128)} %all-gather.2.cloned.1.call-done), kind=kOutput, calls=%fused_computation.6 | convolution fusion | flops 2818572288 | bytes 11141120 | tf_op jit(solution)/shard_map/dot_general | solution.py:15
  252.8 0.0 all-reduce.3.cloned.1.call-update
  252.8 0.2 all-reduce.5.cloned.1.call-start
  253.0 395.9 %all-reduce.3.cloned.1.call-done = f32[128,256]{1,0:T(8,128)} async-done(((f32[128,256]{1,0:T(8,128)}), f32[128,256]{1,0:T(8,128)}) %all-reduce.3.cloned.1.call-update) | async-done | bytes 131088 | tf_op jit(solution)/shard_map/psum | solution.py:35
  649.0 0.0 copy-done.2
  649.0 1.3 fusion.7
  650.3 0.0 copy-start
  650.3 9.2 convolution_subtract_fusion.1
  659.5 0.0 copy-start.1
  659.5 1.8 copy-done.1
  661.3 0.0 copy-done
  661.3 8.1 fusion.1
  669.4 0.0 all-reduce.5.cloned.1.call-update
  669.4 395.6 %all-reduce.5.cloned.1.call-done = f32[128,256]{1,0:T(8,128)} async-done(((f32[128,256]{1,0:T(8,128)}), f32[128,256]{1,0:T(8,128)}) %all-reduce.5.cloned.1.call-update) | async-done | bytes 131088 | tf_op jit(solution)/shard_map/psum | solution.py:35
  1065.0 1.3 fusion.6
  1066.3 10.3 convolution_subtract_fusion
Async XLA Ops:
  6.5 234.0 %all-gather.2.cloned.1.call-start = ((), (), s32[]{:S(2)}) async-start(), calls=%async_computation.1 | async-start | bytes 16515072 | tf_op jit(solution)/shard_map/all_gather | solution.py:32
  7.3 641.7 %all-reduce.3.cloned.1.call-start = ((), (), s32[]{:S(2)}) async-start(), calls=%async_computation.2 | async-start | bytes 262144 | tf_op jit(solution)/shard_map/psum | solution.py:35
  150.4 498.6 %copy-start.2 = (f32[2,256,256]{2,1,0:T(8,128)S(1)}, f32[2,256,256]{2,1,0:T(8,128)}, u32[]{:S(2)}) copy-start(f32[2,256,256]{2,1,0:T(8,128)} %param.5) | copy-start | bytes 1572868
  252.8 812.2 %all-reduce.5.cloned.1.call-start = ((), (), s32[]{:S(2)}) async-start(), calls=%async_computation.3 | async-start | bytes 262144 | tf_op jit(solution)/shard_map/psum | solution.py:35
  650.3 11.1 %copy-start = (f32[7168,512]{0,1:T(8,128)S(1)}, f32[7168,512]{0,1:T(8,128)}, u32[]{:S(2)}) copy-start(f32[7168,512]{0,1:T(8,128)} %all-gather.2.cloned.1.call-done) | copy-start | bytes 44040196
  659.5 1.8 copy-start.1
Sparse Core Ops, SparseCore 0:
  9.1 231.3 all-gather.1
  252.9 396.0 all-reduce.2
  669.5 395.3 all-reduce.4
where the time goes:
time: 1080 us
  waiting for transfers between devices  882 us (82%)
  blocking collectives  138 us (13%)
  matrix products  42.4 us (4%)
  between operations  13.1 us (1%)
    psum x2, waiting for transfers between devices, summer_grid(): return lax.psum(values, 'prow')  792 us
    all_to_all x1, blocking collectives, body(): lax.all_to_all(eigen_rows, 'prow', split_axis=1, concat_axis=0, tiled=True)  138 us
    all_gather x1, waiting for transfers between devices, body(): grid_vectors = lax.all_gather(reflectors, 'pcol', axis=1, tiled=True)  90.1 us
    dot_general x6, matrix products, matmul(): jnp.dot(left, right, precision=lax.Precision.HIGHEST, preferred_element_t...  42.4 us
  transfers between devices with their start and end apart: 3, of which 3 were waited for; matrix products, arithmetic and copies ran while one was open for 0% of the time, Pallas kernels for 0%

commit v1 on v0

v1 whole, which is shorter than its diff:
```python
import jax
import jax.numpy as jnp
from jax import lax
from jax.sharding import PartitionSpec as P


def upper_part(square):
    width = square.shape[0]
    rows = lax.broadcasted_iota(jnp.int32, (width, width), 0)
    cols = lax.broadcasted_iota(jnp.int32, (width, width), 1)
    return jnp.where(cols >= rows, square, jnp.zeros_like(square))


def matmul(left, right, precision=lax.Precision.HIGHEST):
    return jnp.dot(left, right, precision=precision, preferred_element_type=jnp.float32)


def sum_over_prow(values, members):
    slices = values.reshape((members, -1, 128))
    received = lax.all_to_all(slices, "prow", split_axis=0, concat_axis=0, tiled=True)
    total = jnp.sum(received, axis=0, keepdims=True)
    copies = jnp.broadcast_to(total, slices.shape)
    return lax.all_to_all(copies, "prow", split_axis=0, concat_axis=0, tiled=True)


def body(eigen_rows, reflectors, tfactors):
    members = lax.axis_size("prow")
    width = tfactors.shape[1]
    vectors = lax.all_gather(reflectors, "pcol", axis=1, tiled=True)
    rows = lax.all_to_all(eigen_rows, "prow", split_axis=1, concat_axis=0, tiled=True)
    count = rows.shape[0]
    first_tri = upper_part(tfactors[0])
    second_tri = upper_part(tfactors[1])
    fast = lax.Precision.HIGH

    projected = matmul(rows, vectors, fast)
    cross = matmul(vectors[:, width:].T, vectors[:, :width], fast)
    packed = jnp.concatenate(
        [projected.reshape(members, -1), cross.reshape(members, -1)], axis=1
    )
    packed = sum_over_prow(packed, members).reshape(packed.shape)
    split = projected.size // members
    projected = packed[:, :split].reshape(count, 2 * width)
    cross = packed[:, split:].reshape(width, width)
    scaled_second = matmul(projected[:, width:], second_tri.T)
    first = projected[:, :width] - matmul(scaled_second, cross)
    scaled_first = matmul(first, first_tri.T)
    scaled = jnp.concatenate([scaled_first, scaled_second], axis=1)
    return rows - matmul(scaled, vectors.T, fast)


def solution(mesh):
    return jax.shard_map(
        body,
        mesh=mesh,
        in_specs=(P(("pcol", "prow"), None), P("prow", "pcol"), P()),
        out_specs=P("pcol", "prow"),
        check_vma=False,
    )
```

time: 1080 us -> 337 us (0.31)
  waiting for transfers between devices: 882 us -> 90.9 us
  blocking collectives: 138 us -> 184 us
    psum x2 -> x0, waiting for transfers between devices: 792 us -> none  [summer_grid(): return lax.psum(values, 'prow')]
    all_to_all x0 -> x2, blocking collectives: none -> 45.9 us  [the longest x1 27.8 us: sum_over_prow(): lax.all_to_all(slices, 'prow', split_axis=0, concat_axis=0, tiled=True)]
  transfers between devices with their start and end apart: 3 -> 1, of which waited for: 3 -> 1; matrix products, arithmetic and copies ran while one was open for 0% -> 0% of each run, Pallas kernels for 0% -> 0%
where the time goes in v1:
time: 337 us; the launch traced here: 331 us
  blocking collectives  184 us (55%)
  waiting for transfers between devices  90.9 us (27%)
  matrix products  37.4 us (11%)
  between operations  13.5 us (4%)
  local copies, waits for them, and re-layouts  5.81 us (2%)
    all_to_all x1, blocking collectives, body(): lax.all_to_all(eigen_rows, 'prow', split_axis=1, concat_axis=0, tiled=True)  138 us
    all_gather x1, waiting for transfers between devices, body(): vectors = lax.all_gather(reflectors, 'pcol', axis=1, tiled=True)  90.2 us
    dot_general x6, matrix products, matmul(): jnp.dot(left, right, precision=precision, preferred_element_type=jnp.floa...  37.4 us
    all_to_all x1, blocking collectives, sum_over_prow(): lax.all_to_all(slices, 'prow', split_axis=0, concat_axis=0, tiled=True)  27.8 us
    all_to_all x1, blocking collectives, sum_over_prow(): lax.all_to_all(copies, 'prow', split_axis=0, concat_axis=0, tiled=True)  18.1 us
  transfers between devices with their start and end apart: 1, of which 1 were waited for; matrix products, arithmetic and copies ran while one was open for 0% of the time, Pallas kernels for 0%

profile of v1, /device:TPU:2, one launch (start us, length us, event | category | flops | bytes accessed | tf_op | source)
XLA Modules:
  0.0 331.3 jit_solution(14484541034405303866)
XLA Ops:
  6.5 0.0 all-gather.2.cloned.1.call-start
  6.5 0.7 all-gather.2.cloned.1.call-update
  7.3 137.8 %all_to_all.29 = f32[4,32,7168]{2,0,1:T(4,128)} all-to-all(f32[4,32,7168]{2,0,1:T(4,128)} %bitcast.19), channel_id=1, replica_groups=mesh['prow'=32,'pcol'=8] {'prow'}, dimensions={1} | all-to-all | bytes 7340032 | tf_op jit(solution)/shard_map/all_to_all | solution.py:30
  145.0 5.2 %all_to_all.23 = f32[128,7168]{1,0:T(8,128)} reshape(f32[32,4,7168]{2,1,0:T(4,128)} %bitcast.18) | data formatting | bytes 7340032 | tf_op jit(solution)/shard_map/all_to_all | solution.py:30
  150.3 90.2 %all-gather.2.cloned.1.call-done = f32[7168,512]{0,1:T(8,128)} async-done(((f32[7168,64]{0,1:T(8,128)}), f32[7168,512]{0,1:T(8,128)}) %all-gather.2.cloned.1.call-update) | async-done | bytes 14680080 | tf_op jit(solution)/shard_map/all_gather | solution.py:29
  240.5 11.7 %fusion = f32[256,256]{1,0:T(8,128)S(1)} fusion(f32[7168,512]{0,1:T(8,128)} %all-gather.2.cloned.1.call-done), kind=kOutput, calls=%fused_computation.1 | convolution fusion | flops 2818572288 | bytes 14942208 | tf_op jit(solution)/shard_map/dot_general | solution.py:15
  252.2 11.8 %fusion.17 = f32[128,512]{1,0:T(8,128)S(1)} fusion(f32[128,7168]{1,0:T(8,128)} %all_to_all.23, f32[7168,512]{0,1:T(8,128)} %all-gather.2.cloned.1.call-done), kind=kOutput, calls=%fused_computation.24 | convolution fusion | flops 2818572288 | bytes 18612224 | tf_op jit(solution)/shard_map/dot_general | solution.py:15
  264.1 0.0 copy-start
  264.1 0.1 pad_maximum_fusion
  264.1 27.8 %all_to_all.30 = f32[32,32,128]{2,1,0:T(8,128)S(1)} all-to-all(f32[32,32,128]{2,1,0:T(8,128)S(1)} %pad_maximum_fusion), channel_id=1, replica_groups=mesh['prow'=32,'pcol'=8] {'prow'}, dimensions={0} | all-to-all | bytes 1048576 | tf_op jit(solution)/shard_map/all_to_all | solution.py:20
  292.0 0.1 broadcast_in_dim.2
  292.0 18.1 %all_to_all.31 = f32[32,32,128]{2,1,0:T(8,128)S(1)} all-to-all(f32[32,32,128]{2,1,0:T(8,128)S(1)} %broadcast_in_dim.2), channel_id=1, replica_groups=mesh['prow'=32,'pcol'=8] {'prow'}, dimensions={0} | all-to-all | bytes 1048576 | tf_op jit(solution)/shard_map/all_to_all | solution.py:23
  310.1 0.3 copy.7
  310.5 0.1 reshape.21
  310.6 0.0 copy-done
  310.6 0.4 fusion.7
  311.0 0.3 convolution_subtract_fusion.1
  311.3 0.4 fusion.6
  311.7 12.8 %convolution_subtract_fusion = f32[128,7168]{1,0:T(8,128)} fusion(f32[128,7168]{1,0:T(8,128)} %all_to_all.23, f32[7168,512]{0,1:T(8,128)} %all-gather.2.cloned.1.call-done, f32[128,256]{1,0:T(8,128)S(1)} %fusion.7, f32[128,256]{1,0:T(8,128)S(1)} %fusion.6), kind=kOutput, calls=%fused_computation | convolution fusion | flops 2819555328 | bytes 22282240 | tf_op jit(solution)/shard_map/dot_general | solution.py:15
  (5 shorter events, 0.2 us)
Async XLA Ops:
  6.5 233.9 %all-gather.2.cloned.1.call-start = ((), (), s32[]{:S(2)}) async-start(), calls=%async_computation.3 | async-start | bytes 16515072 | tf_op jit(solution)/shard_map/all_gather | solution.py:29
  264.1 46.6 %copy-start = (f32[2,256,256]{2,1,0:T(8,128)S(1)}, f32[2,256,256]{2,1,0:T(8,128)}, u32[]{:S(2)}) copy-start(f32[2,256,256]{2,1,0:T(8,128)} %param.5) | copy-start | bytes 1572868
Sparse Core Ops, SparseCore 0:
  9.1 231.2 all-gather.1
